TPU v7x, 256 devices: a whole 4x4x8 slice. The times are simulated.
256 devices in a mesh: ta: 8 (over x, core), xyz: 32 (over y, z).
Axes of the slice: x: 4, y: 4, z: 8, core: 2. Of those that a mesh axis runs over, the one named last changes fastest.
Arguments:
- nulls: bfloat16 [32, 128, 32, 16, 128], P('ta', 'xyz'), may hold values from -1.1953125 to 1.1953125
- time_links: bfloat16 [16, 128, 32, 64, 128], P('ta', 'xyz'), may hold values from -0.5 to 0.5
- space_links: bfloat16 [32, 64, 32, 64, 128], P('ta', 'xyz'), may hold values from -0.5 to 0.5
- owner_lists: int32 [32, 64], replicated, may hold values from -1 to 1023, as said below
Outputs:
- coarse_links: float32 [8, 2048, 1024], P('ta', 'xyz')
Inputs may be any that keep to these rules, and one draw needn't show every extreme that they name: `owner_lists`: row d lists, in increasing order, the aggregates that shard d owns, followed by -1 in the remaining slots; each of the 1024 aggregate ids appears exactly once. Exactly half of the shards own 64 aggregates each and the others none. The 32 aggregates with ids q * 32 to q * 32 + 31 belong to exactly 8 owners, 4 to each.
All inputs are finite; a program needn't handle non-finite values.
Results may differ from a plain program's by a relative error of at most 0.0029.
Values may be sent and summed in bfloat16 or wider, within the bound.
A program may use at most 64 MiB of HBM per device.

v0:
```python
import jax
import jax.numpy as jnp
from jax import lax
from jax.sharding import PartitionSpec as P


def shifted(array, axis, by):
    count = lax.axis_size(axis)
    return lax.ppermute(array, axis, [(i, (i + by) % count) for i in range(count)])


def forward_image(link_mats, upper_nulls):
    half_width = link_mats.shape[-2]
    upper_real = upper_nulls[..., :half_width]
    upper_imag = upper_nulls[..., half_width:]
    paired = jnp.stack(
        [
            jnp.concatenate([upper_real, -upper_imag], axis=-1),
            jnp.concatenate([upper_imag, upper_real], axis=-1),
        ],
        axis=-3,
    )
    image_pair = jnp.einsum(
        "...ik,...pnk->...pni", link_mats, paired, preferred_element_type=jnp.float32
    )
    joined = jnp.concatenate([image_pair[..., 0, :, :], image_pair[..., 1, :, :]], axis=-1)
    return joined.astype(jnp.bfloat16)


def conjugate_pair(lower_nulls):
    half_width = lower_nulls.shape[-1] // 2
    turned = jnp.concatenate(
        [-lower_nulls[..., half_width:], lower_nulls[..., :half_width]], axis=-1
    )
    return jnp.stack([lower_nulls, turned], axis=-3)


def on_device(nulls, time_links, space_links, owner_lists):
    time_rows, space_rows, side_rows, vectors, doubled = nulls.shape
    time_aggs = time_rows // 2
    space_aggs = space_rows // 2
    side_aggs = side_rows // 4
    local_count = time_aggs * space_aggs * side_aggs
    edge_time = shifted(nulls[0:1], "ta", -1)
    upper_time = jnp.concatenate([nulls[2::2], edge_time], axis=0)
    edge_space = shifted(nulls[:, 0:1], "xyz", -1)
    upper_space = jnp.concatenate([nulls[:, 2::2], edge_space], axis=1)
    image_time = forward_image(time_links, upper_time).reshape(
        time_aggs, space_aggs, 2, side_aggs, 4, vectors, doubled
    )
    pair_time = conjugate_pair(nulls[1::2]).reshape(
        time_aggs, space_aggs, 2, side_aggs, 4, 2, vectors, doubled
    )
    block_time = jnp.einsum(
        "txcaypnk,txcaymk->txapnm", pair_time, image_time, preferred_element_type=jnp.float32
    )
    image_space = forward_image(space_links, upper_space).reshape(
        time_aggs, 2, space_aggs, side_aggs, 4, vectors, doubled
    )
    pair_space = conjugate_pair(nulls[:, 1::2]).reshape(
        time_aggs, 2, space_aggs, side_aggs, 4, 2, vectors, doubled
    )
    block_space = jnp.einsum(
        "tcxaypnk,tcxaymk->txapnm", pair_space, image_space, preferred_element_type=jnp.float32
    )
    block_width = 2 * vectors * vectors
    link_rows = jnp.concatenate(
        [
            block_time.reshape(local_count, block_width),
            block_space.reshape(local_count, block_width),
        ],
        axis=1,
    )
    shard_index = lax.axis_index("xyz")
    my_list = lax.dynamic_index_in_dim(owner_lists, shard_index, 0, keepdims=False)
    present = my_list >= 0
    everything = lax.all_gather(link_rows, "xyz", axis=0, tiled=True)
    picked = everything[jnp.maximum(my_list, 0)]
    result = jnp.where(present[:, None], picked, 0.0)
    return result[None]


def solution(mesh):
    return jax.shard_map(
        on_device,
        mesh=mesh,
        in_specs=(
            P("ta", "xyz", None, None, None),
            P("ta", "xyz", None, None, None),
            P("ta", "xyz", None, None, None),
            P(),
        ),
        out_specs=P("ta", "xyz", None),
        check_vma=False,
    )
```

profile of v0, /device:TPU:2, one launch (start us, length us, event | category | flops | bytes accessed | tf_op | source)
XLA Modules:
  0.0 130.2 jit_solution(7621202235726365997)
XLA Ops:
  6.5 0.0 copy-start
  6.5 0.0 all-gather.2.cloned.1.call-start
  6.5 1.5 %fusion.37 = (bf16[1,4,32,16,128]{4,3,2,1,0:T(8,128)(2,1)S(1)}, bf16[1,4,32,16,128]{4,3,2,1,0:T(8,128)(2,1)S(1)}) fusion(bf16[4,4,32,16,128]{4,3,2,1,0:T(8,128)(2,1)} %param.4), kind=kLoop, calls=%fused_computation.48 | loop fusion | bytes 2097152 | tf_op jit(solution)/shard_map/slice | solution.py:45
  8.1 0.0 collective-permute-start
  8.1 0.3 copy-done
  8.4 1.2 fusion.39
  9.6 8.3 %collective-permute-start.1 = (bf16[4,1,32,16,128]{4,3,2,1,0:T(8,128)(2,1)}, bf16[4,1,32,16,128]{4,3,2,1,0:T(8,128)(2,1)}, u32[]{:S(2)}, u32[]{:S(2)}) collective-permute-start(bf16[4,1,32,16,128]{4,3,2,1,0:T(8,128)(2,1)} %get-tuple-element.12), channel_id=1, source_target_pairs={{0,31},{1,0},{2,1},{3,2},{4,3},{5,4},{6,5},{7,6},{8,7},{9,8},{10,9... | collective-permute-start | bytes 1572872 | tf_op jit(solution)/shard_map/ppermute | solution.py:9
  17.9 0.2 slice.60
  18.1 0.2 slice.69
  18.3 0.4 slice_negate_fusion.1
  18.7 0.6 pad_maximum_fusion.4
  19.3 0.4 slice_negate_fusion
  19.7 0.6 pad_maximum_fusion.5
  20.3 0.0 collective-permute-done
  20.3 0.7 fusion.34
  21.1 0.0 copy-start.1
  21.1 1.2 maximum_bitcast_fusion
  22.2 1.0 copy-done.1
  23.3 2.3 %fusion.14 = bf16[2,4,32,2,16,64]{5,4,3,2,1,0:T(8,128)(2,1)S(1)} fusion(bf16[2,4,32,64,128]{4,3,2,1,0:T(8,128)(2,1)S(1)} %copy-done.1, bf16[2,4,32,1,16,128]{5,4,3,2,1,0:T(8,128)(2,1)S(1)} %get-tuple-element.14, bf16[2,4,32,1,16,128]{5,4,3,2,1,0:T(8,128)(2,1)S(1)} %get-tuple-element.13), kind=kOutput, calls=%fused_computation.17 | convolution fusion | flops 135790592 | bytes 7340032 | tf_op jit(solution)/shard_map/...ik,...pnk->...pni/dot_general | solution.py:23
  25.5 0.6 fusion.36
  26.1 0.0 copy-start.3
  26.1 1.0 fusion.24
  27.1 0.3 reshape.75
  27.4 2.3 %collective-permute-done.1 = bf16[4,1,32,16,128]{4,3,2,1,0:T(8,128)(2,1)} collective-permute-done((bf16[4,1,32,16,128]{4,3,2,1,0:T(8,128)(2,1)}, bf16[4,1,32,16,128]{4,3,2,1,0:T(8,128)(2,1)}, u32[]{:S(2)}, u32[]{:S(2)}) %collective-permute-start.1) | collective-permute-done | bytes 524320 | tf_op jit(solution)/shard_map/ppermute | solution.py:9
  29.7 0.0 copy-done.3
  29.7 1.9 %fusion.35 = (bf16[4,2,32,16,64]{4,3,2,1,0:T(8,128)(2,1)S(1)}, bf16[4,2,32,16,64]{4,3,2,1,0:T(8,128)(2,1)S(1)}, bf16[4,2,32,16,64]{4,3,2,1,0:T(8,128)(2,1)S(1)}) fusion(bf16[4,1,32,16,128]{4,3,2,1,0:T(8,128)(2,1)} %collective-permute-done.1, bf16[4,1,32,16,128]{4,3,2,1,0:T(8,128)(2,1)S(1)} %copy-done.3), kind=kLoop, calls=%fused_computation.46 | loop fusion | flops 2621440 | bytes 2621440 | tf_op jit(solution)/shard_map/neg | solution.py:18
  31.7 0.0 copy-start.2
  31.7 1.2 maximum_bitcast_fusion.3
  32.8 1.0 copy-done.2
  33.9 2.3 %fusion.19 = bf16[4,2,32,2,16,64]{5,4,3,2,1,0:T(8,128)(2,1)S(1)} fusion(bf16[4,2,32,64,128]{4,3,2,1,0:T(8,128)(2,1)S(1)} %copy-done.2, bf16[4,2,32,1,16,128]{5,4,3,2,1,0:T(8,128)(2,1)S(1)} %get-tuple-element.21, bf16[4,2,32,1,16,128]{5,4,3,2,1,0:T(8,128)(2,1)S(1)} %get-tuple-element.20), kind=kOutput, calls=%fused_computation.18 | convolution fusion | flops 135790592 | bytes 7340032 | tf_op jit(solution)/shard_map/...ik,...pnk->...pni/dot_general | solution.py:23
  36.1 0.6 fusion.38
  36.7 1.0 fusion.27
  37.7 0.3 reshape.76
  38.0 0.7 pad_maximum_fusion.6
  38.7 0.0 all-gather.2.cloned.1.call-update
  38.7 0.7 maximum_bitcast_fusion.6
  39.4 0.7 compare_bitcast_fusion
  40.1 79.5 %all-gather.2.cloned.1.call-done = f32[1024,1024]{1,0:T(8,128)} async-done(((f32[32,1024]{1,0:T(8,128)}), f32[1024,1024]{1,0:T(8,128)}) %all-gather.2.cloned.1.call-update) | async-done | bytes 4194320 | tf_op jit(solution)/shard_map/all_gather | solution.py:77
  119.6 3.0 %gather_fusion = f32[64,1024]{1,0:T(8,128)S(1)} fusion(f32[1024,1024]{1,0:T(8,128)} %all-gather.2.cloned.1.call-done, s32[1024]{0:T(1024)S(1)} %pad_clamp_fusion), kind=kCustom, calls=%fused_computation | custom fusion | bytes 524544 | tf_op jit(solution)/shard_map/gather | solution.py:78
  122.5 0.8 bitcast_select_fusion
  (1 shorter events, 0.0 us)
Async XLA Ops:
  6.5 1.9 %copy-start = (bf16[4,4,32,16,128]{4,3,2,1,0:T(8,128)(2,1)S(1)}, bf16[4,4,32,16,128]{4,3,2,1,0:T(8,128)(2,1)}, u32[]{:S(2)}) copy-start(bf16[4,4,32,16,128]{4,3,2,1,0:T(8,128)(2,1)} %param.4) | copy-start | bytes 6291460
  6.5 113.0 %all-gather.2.cloned.1.call-start = ((), (), s32[]{:S(2)}) async-start(), calls=%async_computation | async-start | bytes 4325376 | tf_op jit(solution)/shard_map/all_gather | solution.py:77
  8.1 12.3 %collective-permute-start = (bf16[1,4,32,16,128]{4,3,2,1,0:T(8,128)(2,1)S(1)}, bf16[1,4,32,16,128]{4,3,2,1,0:T(8,128)(2,1)S(1)}, u32[]{:S(2)}, u32[]{:S(2)}) collective-permute-start(bf16[1,4,32,16,128]{4,3,2,1,0:T(8,128)(2,1)S(1)} %get-tuple-element.8), channel_id=1, source_target_pairs={{0,224},{32,0},{64,32},{96,64},{128,96},{160,128},{192,160},{224,1... | collective-permute-start | bytes 1572872 | tf_op jit(solution)/shard_map/ppermute | solution.py:9
  9.6 20.1 %collective-permute-start.1 = (bf16[4,1,32,16,128]{4,3,2,1,0:T(8,128)(2,1)}, bf16[4,1,32,16,128]{4,3,2,1,0:T(8,128)(2,1)}, u32[]{:S(2)}, u32[]{:S(2)}) collective-permute-start(bf16[4,1,32,16,128]{4,3,2,1,0:T(8,128)(2,1)} %get-tuple-element.12), channel_id=1, source_target_pairs={{0,31},{1,0},{2,1},{3,2},{4,3},{5,4},{6,5},{7,6},{8,7},{9,8},{10,9... | collective-permute-start | bytes 1572872 | tf_op jit(solution)/shard_map/ppermute | solution.py:9
  21.1 2.2 %copy-start.1 = (bf16[2,4,32,64,128]{4,3,2,1,0:T(8,128)(2,1)S(1)}, bf16[2,4,32,64,128]{4,3,2,1,0:T(8,128)(2,1)}, u32[]{:S(2)}) copy-start(bf16[2,4,32,64,128]{4,3,2,1,0:T(8,128)(2,1)} %param.5) | copy-start | bytes 12582916
  26.1 3.6 %copy-start.3 = (bf16[4,1,32,16,128]{4,3,2,1,0:T(8,128)(2,1)S(1)}, bf16[4,1,32,16,128]{4,3,2,1,0:T(8,128)(2,1)}, u32[]{:S(2)}) copy-start(bf16[4,1,32,16,128]{4,3,2,1,0:T(8,128)(2,1)} %get-tuple-element.11) | copy-start | bytes 1572868
  31.7 2.2 %copy-start.2 = (bf16[4,2,32,64,128]{4,3,2,1,0:T(8,128)(2,1)S(1)}, bf16[4,2,32,64,128]{4,3,2,1,0:T(8,128)(2,1)}, u32[]{:S(2)}) copy-start(bf16[4,2,32,64,128]{4,3,2,1,0:T(8,128)(2,1)} %param.6) | copy-start | bytes 12582916
Sparse Core Ops, SparseCore 0:
  38.8 80.7 all-gather.1
where the time goes:
time: 130 us
  waiting for transfers between devices  81.8 us (63%)
  between operations  13.5 us (10%)
  local copies, waits for them, and re-layouts  10.1 us (8%)
  other arithmetic  9.83 us (8%)
  starting transfers between devices  8.33 us (6%)
  matrix products  6.58 us (5%)
    all_gather x1, waiting for transfers between devices, on_device(): everything = lax.all_gather(link_rows, 'xyz', axis=0, tiled=True)  79.5 us
    ppermute x2, starting transfers between devices, shifted(): lax.ppermute(array, axis, [(i, (i + by) % count) for i in range(count)])  8.32 us
    dot_general x2, matrix products, forward_image(): jnp.einsum('...ik,...pnk->...pni', link_mats, paired, preferred_element_t...  4.55 us
    gather x1, local copies, waits for them, and re-layouts, on_device(): picked = everything[jnp.maximum(my_list, 0)]  2.98 us
    neg x2, other arithmetic, forward_image(): -upper_imag  2.63 us
  transfers between devices with their start and end apart: 3, of which 2 were waited for; matrix products, arithmetic and copies ran while one was open for 8% of the time, Pallas kernels for 0%

commit v1 on v0

v1 whole, which is shorter than its diff:
```python
import functools

import jax
import jax.numpy as jnp
from jax import lax
from jax.experimental import pallas as pl
from jax.experimental.pallas import tpu as pltpu
from jax.sharding import PartitionSpec as P

MESH = pl.DeviceIdType.MESH
NY, NZ = 4, 8
BF, F32, I32 = jnp.bfloat16, jnp.float32, jnp.int32


def dot_nt(a, b):
    return lax.dot_general(a, b, (((1,), (1,)), ((), ())), preferred_element_type=F32)


def dot_nn(a, b):
    return lax.dot_general(a, b, (((1,), (0,)), ((), ())), preferred_element_type=F32)


def iota(shape, dim):
    return lax.broadcasted_iota(I32, shape, dim)


def one_hot(cond):
    return jnp.where(cond, 1.0, 0.0).astype(BF)


def swap_halves(x):
    return jnp.concatenate([x[:, 64:], x[:, :64]], axis=1)


def kernel(
    nulls_hbm, tl_hbm, sl_hbm, owner_ref, out_ref,
    nulls, tl, sl, th, sh, zm, group_rows, pack, unpack, send, recv,
    nulls_sem, link_sem, halo_send, halo_recv, row_send, row_recv, own_sem,
):
    ta = lax.axis_index("ta")
    me = lax.axis_index("xyz")
    n_ta, n_xyz = 8, NY * NZ
    my_y, my_z = me // NZ, me % NZ
    ta_down, ta_up = (ta + n_ta - 1) % n_ta, (ta + 1) % n_ta
    down = (me + n_xyz - 1) % n_xyz

    def peer(k):
        kz, ky = k // NY, k % NY
        half = kz // 2 + kz % 2
        dz = jnp.where(kz == 7, 0, jnp.where(kz % 2 == 1, 4 + half, 4 - half))
        dy = jnp.where(ky == 3, 0, jnp.where(ky % 2 == 1, 3, 2 - ky // 2))
        return ((my_y + dy) % NY) * NZ + (my_z + dz) % NZ

    barrier = pltpu.get_barrier_semaphore()
    pl.semaphore_signal(barrier, inc=1, device_id={"ta": ta_down}, device_id_type=MESH)
    pl.semaphore_signal(barrier, inc=1, device_id={"ta": ta_up}, device_id_type=MESH)

    @pl.loop(0, n_xyz - 1)
    def _(k):
        pl.semaphore_signal(barrier, inc=1, device_id={"xyz": peer(k)}, device_id_type=MESH)

    nulls_copy = pltpu.make_async_copy(nulls_hbm, nulls, nulls_sem)
    nulls_copy.start()
    groups = [("t", 0, 0), ("t", 0, 1), ("s", 0, 0), ("s", 1, 0), ("t", 1, 0), ("t", 1, 1), ("s", 0, 1), ("s", 1, 1)]
    link_copies = {}
    for i, (kind, at, ax) in enumerate(groups):
        if kind == "t":
            src, dst = tl_hbm.at[at, pl.ds(2 * ax, 2)], tl.at[at, pl.ds(2 * ax, 2)]
        else:
            src, dst = sl_hbm.at[pl.ds(2 * at, 2), ax], sl.at[pl.ds(2 * at, 2), ax]
        link_copies[kind, at, ax] = pltpu.make_async_copy(src, dst, link_sem.at[i])
        link_copies[kind, at, ax].start()

    pl.semaphore_wait(barrier, n_xyz + 1)

    halo = {}
    for part in range(2):
        halo["s", part] = pltpu.make_async_remote_copy(
            nulls_hbm.at[pl.ds(2 * part, 2), 0], sh.at[pl.ds(2 * part, 2)],
            halo_send.at[2 + part], halo_recv.at[2 + part], device_id={"xyz": down}, device_id_type=MESH)
        halo["t", part] = pltpu.make_async_remote_copy(
            nulls_hbm.at[0, pl.ds(2 * part, 2)], th.at[pl.ds(2 * part, 2)],
            halo_send.at[part], halo_recv.at[part], device_id={"ta": ta_down}, device_id_type=MESH)
        halo["s", part].start()
        halo["t", part].start()

    row, col = iota((128, 1024), 0), iota((128, 1024), 1)
    group_rows[...] = one_hot(((row % 32) == (col // 32)) & ((row // 32) == ((col // 8) % 4)))
    lists = owner_ref[...]
    wide = jnp.broadcast_to(lists[:, None, :], (32, 16, 64)).reshape(512, 64)
    base = me * 32
    first = jnp.sum(jnp.where((wide >= 0) & (wide < base), 1, 0), axis=1, keepdims=True)
    r512 = iota((512, 1), 0)
    agg = jnp.sum(jnp.where(iota((512, 64), 1) == first + r512 % 4, wide, 0), axis=1, keepdims=True) - base
    target = jnp.where((agg >= 0) & (agg < 32), ((r512 // 4) % 4) * 32 + agg, -1)
    pack[...] = one_hot(iota((512, 128), 1) == target)
    mine = jnp.broadcast_to(owner_ref[pl.ds(me, 1), :], (256, 64))
    r256 = iota((256, 1), 0)
    slot = r256 % 64
    listed = jnp.sum(jnp.where(iota((256, 64), 1) == slot, mine, 0), axis=1, keepdims=True)
    place = jnp.where(listed >= 0, (listed // 32) * 16 + (r256 // 64) * 4 + slot % 4, -1)
    unpack[...] = one_hot(iota((256, 512), 1) == place)

    lane = iota((16, 128), 1)
    low16 = lane < 64
    low32 = iota((32, 128), 1) < 64
    spread = one_hot(iota((16, 128), 0) == iota((16, 128), 1) % 16)
    keep = (iota((32, 128), 1) // 16) == (iota((32, 128), 0) % 8)

    def aggregate(half, agg, links, uppers, lowers):
        left, right = [], []
        for c in range(2):
            for w in range(0, 4, 2):
                a, b = uppers(c, w), uppers(c, w + 1)
                sa, sb = jnp.where(low16, a, -a), jnp.where(low16, b, -b)
                paired = jnp.concatenate([sa, swap_halves(a), sb, swap_halves(b)], axis=0)
                product = dot_nt(paired, links(c, w))
                image = jnp.where(low32, product[:32], product[32:]).astype(BF)
                right.append(image[:16])
                right.append(image[16:])
                la, lb = lowers(c, w), lowers(c, w + 1)
                re = jnp.where(low16, la, swap_halves(lb))
                im = jnp.where(low16, swap_halves(la), lb)
                left.append(jnp.concatenate([re, -im], axis=0))
                left.append(jnp.concatenate([im, re], axis=0))
        block = dot_nt(jnp.concatenate(left, axis=1), jnp.concatenate(right, axis=1))
        tiled = dot_nn(block.astype(BF), spread)
        zm[half, pl.ds(agg * 32, 32), :] = jnp.where(keep, tiled, 0.0).astype(BF)

    def group(kind, at, ax):
        link_copies[kind, at, ax].wait()

        def body(aw, _):
            w0 = aw * 4
            if kind == "t":
                def links(c, w):
                    return tl[at, 2 * ax + c, pl.ds(w0 + w, 2)].reshape(128, 128)

                def uppers(c, w):
                    return nulls[2, 2 * ax + c, w0 + w] if at == 0 else th[2 * ax + c, w0 + w]

                def lowers(c, w):
                    return nulls[2 * at + 1, 2 * ax + c, w0 + w]
            else:
                def links(c, w):
                    return sl[2 * at + c, ax, pl.ds(w0 + w, 2)].reshape(128, 128)

                def uppers(c, w):
                    return nulls[2 * at + c, 2, w0 + w] if ax == 0 else sh[2 * at + c, w0 + w]

                def lowers(c, w):
                    return nulls[2 * at + c, 2 * ax + 1, w0 + w]
            aggregate(0 if kind == "t" else 1, (at * 2 + ax) * 8 + aw, links, uppers, lowers)
            return 0

        lax.fori_loop(0, 8, body, 0, unroll=2)

    def row_copy(half, to, slot):
        return pltpu.make_async_remote_copy(
            send.at[half, to], recv.at[half, me], row_send.at[half, to], row_recv.at[half, slot],
            device_id={"xyz": to}, device_id_type=MESH)

    def deliver(half):
        rows = dot_nn(group_rows[...], zm[half]).astype(BF)
        send[half] = dot_nn(pack[...], rows).astype(BF).reshape(n_xyz, 16, 128)

        @pl.loop(0, n_xyz - 1)
        def _(k):
            row_copy(half, peer(k), me).start()

        pltpu.make_async_copy(send.at[half, me], recv.at[half, me], own_sem.at[half]).start()

    def collect(half):
        pltpu.make_async_copy(send.at[half, me], recv.at[half, me], own_sem.at[half]).wait()

        @pl.loop(0, n_xyz - 1)
        def _(k):
            to = peer(k)
            row_copy(half, to, to).wait()

        placed = dot_nn(unpack[...], recv[half].reshape(512, 128))
        for q in range(4):
            out_ref[:, half * 512 + q * 128:half * 512 + (q + 1) * 128] = placed[q * 64:(q + 1) * 64]

    nulls_copy.wait()
    group("t", 0, 0)
    group("t", 0, 1)
    group("s", 0, 0)
    group("s", 1, 0)
    halo["t", 0].wait()
    group("t", 1, 0)
    halo["t", 1].wait()
    group("t", 1, 1)
    deliver(0)
    halo["s", 0].wait()
    group("s", 0, 1)
    halo["s", 1].wait()
    group("s", 1, 1)
    deliver(1)
    collect(0)
    collect(1)


def on_device(nulls, time_links, space_links, owner_lists):
    result = pl.pallas_call(
        kernel,
        out_shape=jax.ShapeDtypeStruct((64, 1024), F32),
        in_specs=[pl.BlockSpec(memory_space=pl.ANY)] * 3 + [pl.BlockSpec(memory_space=pltpu.VMEM)],
        out_specs=pl.BlockSpec(memory_space=pltpu.VMEM),
        scratch_shapes=[
            pltpu.VMEM((4, 4, 32, 16, 128), BF),
            pltpu.VMEM((2, 4, 32, 64, 128), BF),
            pltpu.VMEM((4, 2, 32, 64, 128), BF),
            pltpu.VMEM((4, 32, 16, 128), BF),
            pltpu.VMEM((4, 32, 16, 128), BF),
            pltpu.VMEM((2, 1024, 128), BF),
            pltpu.VMEM((128, 1024), BF),
            pltpu.VMEM((512, 128), BF),
            pltpu.VMEM((256, 512), BF),
            pltpu.VMEM((2, 32, 16, 128), BF),
            pltpu.VMEM((2, 32, 16, 128), BF),
            pltpu.SemaphoreType.DMA,
            pltpu.SemaphoreType.DMA((8,)),
            pltpu.SemaphoreType.DMA((4,)),
            pltpu.SemaphoreType.DMA((4,)),
            pltpu.SemaphoreType.DMA((2, 32)),
            pltpu.SemaphoreType.DMA((2, 32)),
            pltpu.SemaphoreType.DMA((2,)),
        ],
        compiler_params=pltpu.CompilerParams(collective_id=0, has_side_effects=True),
    )(nulls, time_links, space_links, owner_lists)
    return result[None]


def solution(mesh):
    return jax.shard_map(
        on_device,
        mesh=mesh,
        in_specs=(
            P("ta", "xyz", None, None, None),
            P("ta", "xyz", None, None, None),
            P("ta", "xyz", None, None, None),
            P(),
        ),
        out_specs=P("ta", "xyz", None),
        check_vma=False,
    )
```

time: 130 us -> 50 us (0.38)
  waiting for transfers between devices: 81.8 us -> 0 us
  Pallas kernels: 0 us -> 48.1 us
  between operations: 13.5 us -> 0.01 us
  other arithmetic: 9.83 us -> 0 us
  local copies, waits for them, and re-layouts: 10.1 us -> 1.67 us
  starting transfers between devices: 8.33 us -> 0 us
  matrix products: 6.58 us -> 0 us
    all_gather x1 -> x0, waiting for transfers between devices: 79.5 us -> none  [on_device(): everything = lax.all_gather(link_rows, 'xyz', axis=0, tiled=True)]
    pallas_call x0 -> x1, Pallas kernels: none -> 48.1 us  [on_device(): pl.pallas_call(kernel, out_shape=jax.ShapeDtypeStruct((64, 1024), F32), i...]
    ppermute x2 -> x0, starting transfers between devices: 8.32 us -> none  [shifted(): lax.ppermute(array, axis, [(i, (i + by) % count) for i in range(count)])]
    dot_general x4 -> x0, matrix products: 6.58 us -> none  [the longest x2 4.55 us: forward_image(): jnp.einsum('...ik,...pnk->...pni', link_mats, paired, preferred_element_t...]
    slice x6 -> x0, local copies, waits for them, and re-layouts: 4.17 us -> none  [the longest x1 1.53 us: on_device(): upper_time = jnp.concatenate([nulls[2::2], edge_time], axis=0)]
    neg x4 -> x0, other arithmetic: 3.5 us -> none  [the longest x2 2.63 us: forward_image(): -upper_imag]
    gather x1 -> x0, local copies, waits for them, and re-layouts: 2.98 us -> none  [on_device(): picked = everything[jnp.maximum(my_list, 0)]]
    ppermute x2 -> x0, waiting for transfers between devices: 2.34 us -> none  [shifted(): lax.ppermute(array, axis, [(i, (i + by) % count) for i in range(count)])]
  transfers between devices with their start and end apart: 3 -> 0, of which waited for: 2 -> 0; matrix products, arithmetic and copies ran while one was open for 8% -> 0% of each run, Pallas kernels for 0% -> 0%
where the time goes in v1:
time: 50 us; the launch traced here: 49.8 us
  Pallas kernels  48.1 us (96%)
  local copies, waits for them, and re-layouts  1.67 us (3%)
    pallas_call x1, Pallas kernels, on_device(): pl.pallas_call(kernel, out_shape=jax.ShapeDtypeStruct((64, 1024), F32), i...  48.1 us
    unnamed x1, local copies, waits for them, and re-layouts  1.67 us

profile of v1, /device:TPU:2, one launch (start us, length us, event | category | flops | bytes accessed | tf_op | source)
XLA Modules:
  0.0 49.8 jit_solution(18166615585760310936)
XLA Ops:
  0.0 48.1 %shard_map.46 = f32[64,1024]{1,0:T(8,128)} custom-call(bf16[4,4,32,16,128]{4,3,2,1,0:T(8,128)(2,1)} %nulls_hbm.1, bf16[2,4,32,64,128]{4,3,2,1,0:T(8,128)(2,1)} %tl_hbm.1, bf16[4,2,32,64,128]{4,3,2,1,0:T(8,128)(2,1)} %sl_hbm.1, s32[32,64]{1,0:T(8,128)} %owner_ref.1), custom_call_target="tpu_custom_call" | custom-call | tf_op jit(solution)/shard_map/pallas_call | solution.py:205
  48.1 1.7 %copy.6 = f32[1,64,1024]{2,1,0:T(8,128)} copy(f32[1,64,1024]{2,1,0:T(8,128)} %bitcast.1) | data formatting | bytes 524288

commit v2 on v1

--- a/solution.py
+++ b/solution.py
@@ -34,7 +34,7 @@
 
 def kernel(
     nulls_hbm, tl_hbm, sl_hbm, owner_ref, out_ref,
-    nulls, tl, sl, th, sh, zm, group_rows, pack, unpack, send, recv,
+    nulls, tl, sl, th, sh, held, row_parts, group_rows, pack, unpack, send, recv,
     nulls_sem, link_sem, halo_send, halo_recv, row_send, row_recv, own_sem,
 ):
     ta = lax.axis_index("ta")
@@ -84,8 +84,8 @@
         halo["s", part].start()
         halo["t", part].start()
 
-    row, col = iota((128, 1024), 0), iota((128, 1024), 1)
-    group_rows[...] = one_hot(((row % 32) == (col // 32)) & ((row // 32) == ((col // 8) % 4)))
+    row, col = iota((32, 256), 0), iota((32, 256), 1)
+    group_rows[...] = one_hot(((row % 8) == (col // 32)) & ((row // 8) == ((col // 8) % 4)))
     lists = owner_ref[...]
     wide = jnp.broadcast_to(lists[:, None, :], (32, 16, 64)).reshape(512, 64)
     base = me * 32
@@ -101,59 +101,69 @@
     place = jnp.where(listed >= 0, (listed // 32) * 16 + (r256 // 64) * 4 + slot % 4, -1)
     unpack[...] = one_hot(iota((256, 512), 1) == place)
 
-    lane = iota((16, 128), 1)
-    low16 = lane < 64
+    low16 = iota((16, 128), 1) < 64
     low32 = iota((32, 128), 1) < 64
+    turn = jnp.where(low16, 1.0, -1.0).astype(BF)
     spread = one_hot(iota((16, 128), 0) == iota((16, 128), 1) % 16)
-    keep = (iota((32, 128), 1) // 16) == (iota((32, 128), 0) % 8)
-
-    def aggregate(half, agg, links, uppers, lowers):
-        left, right = [], []
-        for c in range(2):
-            for w in range(0, 4, 2):
-                a, b = uppers(c, w), uppers(c, w + 1)
-                sa, sb = jnp.where(low16, a, -a), jnp.where(low16, b, -b)
-                paired = jnp.concatenate([sa, swap_halves(a), sb, swap_halves(b)], axis=0)
-                product = dot_nt(paired, links(c, w))
-                image = jnp.where(low32, product[:32], product[32:]).astype(BF)
-                right.append(image[:16])
-                right.append(image[16:])
-                la, lb = lowers(c, w), lowers(c, w + 1)
-                re = jnp.where(low16, la, swap_halves(lb))
-                im = jnp.where(low16, swap_halves(la), lb)
-                left.append(jnp.concatenate([re, -im], axis=0))
-                left.append(jnp.concatenate([im, re], axis=0))
-        block = dot_nt(jnp.concatenate(left, axis=1), jnp.concatenate(right, axis=1))
-        tiled = dot_nn(block.astype(BF), spread)
-        zm[half, pl.ds(agg * 32, 32), :] = jnp.where(keep, tiled, 0.0).astype(BF)
+    keep = (iota((256, 128), 1) // 16) == (iota((256, 128), 0) % 8)
+    none = jnp.zeros((32, 128), BF)
+
+    def images(c, w, links, uppers):
+        mats = links(c, w)
+        weights = jnp.concatenate(
+            [jnp.concatenate([mats[0], mats[2]], axis=0), jnp.concatenate([mats[1], mats[3]], axis=0)], axis=1)
+        rows = []
+        for i in range(4):
+            v = uppers(c, w + i)
+            paired = jnp.concatenate([v * turn, swap_halves(v)], axis=0)
+            rows.append(jnp.concatenate([none, paired] if i % 2 else [paired, none], axis=1))
+        product = dot_nt(jnp.concatenate(rows, axis=0), weights)
+        for i in range(2):
+            yield jnp.where(low32, product[32 * i:32 * i + 32], product[64 + 32 * i:96 + 32 * i]).astype(BF)
+
+    def conjugates(c, w, lowers):
+        for i in range(2):
+            a, b = lowers(c, w + i), lowers(c, w + i + 2)
+            re = jnp.where(low16, a, swap_halves(b))
+            im = jnp.where(low16, swap_halves(a), b)
+            yield jnp.concatenate([re, -im], axis=0)
+            yield jnp.concatenate([im, re], axis=0)
 
     def group(kind, at, ax):
-        link_copies[kind, at, ax].wait()
-
-        def body(aw, _):
-            w0 = aw * 4
-            if kind == "t":
-                def links(c, w):
-                    return tl[at, 2 * ax + c, pl.ds(w0 + w, 2)].reshape(128, 128)
-
-                def uppers(c, w):
-                    return nulls[2, 2 * ax + c, w0 + w] if at == 0 else th[2 * ax + c, w0 + w]
-
-                def lowers(c, w):
-                    return nulls[2 * at + 1, 2 * ax + c, w0 + w]
-            else:
-                def links(c, w):
-                    return sl[2 * at + c, ax, pl.ds(w0 + w, 2)].reshape(128, 128)
-
-                def uppers(c, w):
-                    return nulls[2 * at + c, 2, w0 + w] if ax == 0 else sh[2 * at + c, w0 + w]
-
-                def lowers(c, w):
-                    return nulls[2 * at + c, 2 * ax + 1, w0 + w]
-            aggregate(0 if kind == "t" else 1, (at * 2 + ax) * 8 + aw, links, uppers, lowers)
-            return 0
-
-        lax.fori_loop(0, 8, body, 0, unroll=2)
+        if kind == "t":
+            def links(c, w):
+                return [tl[at, 2 * ax + c, w + i] for i in range(4)]
+
+            def uppers(c, w):
+                return nulls[2, 2 * ax + c, w] if at == 0 else th[2 * ax + c, w]
+
+            def lowers(c, w):
+                return nulls[2 * at + 1, 2 * ax + c, w]
+        else:
+            def links(c, w):
+                return [sl[2 * at + c, ax, w + i] for i in range(4)]
+
+            def uppers(c, w):
+                return nulls[2 * at + c, 2, w] if ax == 0 else sh[2 * at + c, w]
+
+            def lowers(c, w):
+                return nulls[2 * at + c, 2 * ax + 1, w]
+        slot = (at * 2 + ax) + (0 if kind == "t" else 4)
+        for aw in range(8):
+            for c in range(2):
+                for i, image in enumerate(images(c, 4 * aw, links, uppers)):
+                    k = (c * 2 + i) * 256
+                    held[slot, aw, :, k:k + 128] = image[:16]
+                    held[slot, aw, :, k + 128:k + 256] = image[16:]
+        blocks = []
+        for aw in range(8):
+            left = jnp.concatenate([x for c in range(2) for x in conjugates(c, 4 * aw, lowers)], axis=1)
+            blocks.append(dot_nt(left, held[slot, aw]))
+        tiled = dot_nn(jnp.concatenate(blocks, axis=0).astype(BF), spread)
+        rows = dot_nn(group_rows[...], jnp.where(keep, tiled, 0.0).astype(BF))
+        half = 0 if kind == "t" else 1
+        for q in range(4):
+            row_parts[half, pl.ds(q * 32 + (at * 2 + ax) * 8, 8), :] = rows[8 * q:8 * q + 8]
 
     def row_copy(half, to, slot):
         return pltpu.make_async_remote_copy(
@@ -161,8 +171,7 @@
             device_id={"xyz": to}, device_id_type=MESH)
 
     def deliver(half):
-        rows = dot_nn(group_rows[...], zm[half]).astype(BF)
-        send[half] = dot_nn(pack[...], rows).astype(BF).reshape(n_xyz, 16, 128)
+        send[half] = dot_nn(pack[...], row_parts[half].astype(BF)).astype(BF).reshape(n_xyz, 16, 128)
 
         @pl.loop(0, n_xyz - 1)
         def _(k):
@@ -183,6 +192,8 @@
             out_ref[:, half * 512 + q * 128:half * 512 + (q + 1) * 128] = placed[q * 64:(q + 1) * 64]
 
     nulls_copy.wait()
+    for key in groups:
+        link_copies[key].wait()
     group("t", 0, 0)
     group("t", 0, 1)
     group("s", 0, 0)
@@ -213,8 +224,9 @@
             pltpu.VMEM((4, 2, 32, 64, 128), BF),
             pltpu.VMEM((4, 32, 16, 128), BF),
             pltpu.VMEM((4, 32, 16, 128), BF),
-            pltpu.VMEM((2, 1024, 128), BF),
-            pltpu.VMEM((128, 1024), BF),
+            pltpu.VMEM((8, 8, 16, 1024), BF),
+            pltpu.VMEM((2, 128, 128), F32),
+            pltpu.VMEM((32, 256), BF),
             pltpu.VMEM((512, 128), BF),
             pltpu.VMEM((256, 512), BF),
             pltpu.VMEM((2, 32, 16, 128), BF),

time: 50 us -> 37.2 us (0.74)
  Pallas kernels: 48.1 us -> 35.4 us
    pallas_call x1, Pallas kernels: 48.1 us -> 35.4 us  [on_device(): pl.pallas_call(kernel, out_shape=jax.ShapeDtypeStruct((64, 1024), F32), i...]
where the time goes in v2:
time: 37.2 us; the launch traced here: 37.1 us
  Pallas kernels  35.4 us (95%)
  local copies, waits for them, and re-layouts  1.67 us (4%)
    pallas_call x1, Pallas kernels, on_device(): pl.pallas_call(kernel, out_shape=jax.ShapeDtypeStruct((64, 1024), F32), i...  35.4 us
    unnamed x1, local copies, waits for them, and re-layouts  1.67 us

profile of v2, /device:TPU:2, one launch (start us, length us, event | category | flops | bytes accessed | tf_op | source)
XLA Modules:
  0.0 37.1 jit_solution(11311132174912525215)
XLA Ops:
  0.0 35.4 %shard_map.46 = f32[64,1024]{1,0:T(8,128)} custom-call(bf16[4,4,32,16,128]{4,3,2,1,0:T(8,128)(2,1)} %nulls_hbm.1, bf16[2,4,32,64,128]{4,3,2,1,0:T(8,128)(2,1)} %tl_hbm.1, bf16[4,2,32,64,128]{4,3,2,1,0:T(8,128)(2,1)} %sl_hbm.1, s32[32,64]{1,0:T(8,128)} %owner_ref.1), custom_call_target="tpu_custom_call" | custom-call | tf_op jit(solution)/shard_map/pallas_call | solution.py:216
  35.4 1.7 %copy.6 = f32[1,64,1024]{2,1,0:T(8,128)} copy(f32[1,64,1024]{2,1,0:T(8,128)} %bitcast.1) | data formatting | bytes 524288

commit v3 on v2

--- a/solution.py
+++ b/solution.py
@@ -34,34 +34,29 @@
 
 def kernel(
     nulls_hbm, tl_hbm, sl_hbm, owner_ref, out_ref,
-    nulls, tl, sl, th, sh, held, row_parts, group_rows, pack, unpack, send, recv,
+    nulls, tl, sl, th, sh, held, row_parts, through, back, group_rows, pack, unpack, send, recv,
     nulls_sem, link_sem, halo_send, halo_recv, row_send, row_recv, own_sem,
 ):
     ta = lax.axis_index("ta")
     me = lax.axis_index("xyz")
     n_ta, n_xyz = 8, NY * NZ
-    my_y, my_z = me // NZ, me % NZ
-    ta_down, ta_up = (ta + n_ta - 1) % n_ta, (ta + 1) % n_ta
-    down = (me + n_xyz - 1) % n_xyz
-
-    def peer(k):
-        kz, ky = k // NY, k % NY
-        half = kz // 2 + kz % 2
-        dz = jnp.where(kz == 7, 0, jnp.where(kz % 2 == 1, 4 + half, 4 - half))
-        dy = jnp.where(ky == 3, 0, jnp.where(ky % 2 == 1, 3, 2 - ky // 2))
-        return ((my_y + dy) % NY) * NZ + (my_z + dz) % NZ
+    ta_down, ta_up = lax.rem(ta + n_ta - 1, n_ta), lax.rem(ta + 1, n_ta)
+    down, up = lax.rem(me + n_xyz - 1, n_xyz), lax.rem(me + 1, n_xyz)
+    my_y, my_z = lax.div(me, NZ), lax.rem(me, NZ)
+    rows_y = [lax.rem(my_y + dy, NY) * NZ for dy in range(NY)]
+    rows_z = [lax.rem(my_z + dz, NZ) for dz in range(NZ)]
+    peers = [rows_y[dy] + rows_z[dz] for dz in (4, 3, 5, 2, 6, 1, 7, 0) for dy in (2, 1, 3, 0)][:-1]
 
     barrier = pltpu.get_barrier_semaphore()
     pl.semaphore_signal(barrier, inc=1, device_id={"ta": ta_down}, device_id_type=MESH)
     pl.semaphore_signal(barrier, inc=1, device_id={"ta": ta_up}, device_id_type=MESH)
 
-    @pl.loop(0, n_xyz - 1)
-    def _(k):
-        pl.semaphore_signal(barrier, inc=1, device_id={"xyz": peer(k)}, device_id_type=MESH)
+    for peer in peers:
+        pl.semaphore_signal(barrier, inc=1, device_id={"xyz": peer}, device_id_type=MESH)
 
     nulls_copy = pltpu.make_async_copy(nulls_hbm, nulls, nulls_sem)
     nulls_copy.start()
-    groups = [("t", 0, 0), ("t", 0, 1), ("s", 0, 0), ("s", 1, 0), ("t", 1, 0), ("t", 1, 1), ("s", 0, 1), ("s", 1, 1)]
+    groups = [("s", 1, 1), ("t", 0, 0), ("t", 0, 1), ("s", 0, 0), ("s", 1, 0), ("t", 1, 0), ("t", 1, 1), ("s", 0, 1)]
     link_copies = {}
     for i, (kind, at, ax) in enumerate(groups):
         if kind == "t":
@@ -70,19 +65,6 @@
             src, dst = sl_hbm.at[pl.ds(2 * at, 2), ax], sl.at[pl.ds(2 * at, 2), ax]
         link_copies[kind, at, ax] = pltpu.make_async_copy(src, dst, link_sem.at[i])
         link_copies[kind, at, ax].start()
-
-    pl.semaphore_wait(barrier, n_xyz + 1)
-
-    halo = {}
-    for part in range(2):
-        halo["s", part] = pltpu.make_async_remote_copy(
-            nulls_hbm.at[pl.ds(2 * part, 2), 0], sh.at[pl.ds(2 * part, 2)],
-            halo_send.at[2 + part], halo_recv.at[2 + part], device_id={"xyz": down}, device_id_type=MESH)
-        halo["t", part] = pltpu.make_async_remote_copy(
-            nulls_hbm.at[0, pl.ds(2 * part, 2)], th.at[pl.ds(2 * part, 2)],
-            halo_send.at[part], halo_recv.at[part], device_id={"ta": ta_down}, device_id_type=MESH)
-        halo["s", part].start()
-        halo["t", part].start()
 
     row, col = iota((32, 256), 0), iota((32, 256), 1)
     group_rows[...] = one_hot(((row % 8) == (col // 32)) & ((row // 8) == ((col // 8) % 4)))
@@ -129,6 +111,42 @@
             yield jnp.concatenate([re, -im], axis=0)
             yield jnp.concatenate([im, re], axis=0)
 
+    def merge(blocks):
+        tiled = dot_nn(jnp.concatenate(blocks, axis=0).astype(BF), spread)
+        return dot_nn(group_rows[...], jnp.where(keep, tiled, 0.0).astype(BF))
+
+    def place(half, part, rows):
+        for q in range(4):
+            row_parts[half, pl.ds(q * 32 + part * 8, 8), :] = rows[8 * q:8 * q + 8]
+
+    def conjugate_through():
+        zero = jnp.zeros((16, 128), BF)
+        for c in range(2):
+            for w in range(0, 32, 4):
+                rows = []
+                for i in range(4):
+                    v = nulls[2 + c, 3, w + i]
+                    t = swap_halves(v)
+                    if i % 2 == 0:
+                        part = jnp.concatenate([jnp.where(low16, v, zero), jnp.where(low16, t, zero)], axis=0)
+                    else:
+                        part = jnp.concatenate([jnp.where(low16, zero, t), jnp.where(low16, zero, v)], axis=0)
+                    rows.append(jnp.concatenate([part, none] if i < 2 else [none, part], axis=1))
+                weights = jnp.concatenate([sl[2 + c, 1, w + i] for i in range(4)], axis=0)
+                product = dot_nn(jnp.concatenate(rows, axis=0), weights)
+                for i in range(4):
+                    top, low = product[32 * i:32 * i + 16], product[32 * i + 16:32 * i + 32]
+                    through[0, c, w + i] = (top + jnp.where(low16, swap_halves(low), -swap_halves(low))).astype(BF)
+
+    def blocks_through(aw):
+        left, right = [], []
+        for c in range(2):
+            for w in range(4 * aw, 4 * aw + 4):
+                v = through[1, c, w]
+                left.append(jnp.concatenate([v * turn, swap_halves(v)], axis=0))
+                right.append(nulls[2 + c, 0, w])
+        return dot_nt(jnp.concatenate(left, axis=1), jnp.concatenate(right, axis=1))
+
     def group(kind, at, ax):
         if kind == "t":
             def links(c, w):
@@ -159,11 +177,7 @@
         for aw in range(8):
             left = jnp.concatenate([x for c in range(2) for x in conjugates(c, 4 * aw, lowers)], axis=1)
             blocks.append(dot_nt(left, held[slot, aw]))
-        tiled = dot_nn(jnp.concatenate(blocks, axis=0).astype(BF), spread)
-        rows = dot_nn(group_rows[...], jnp.where(keep, tiled, 0.0).astype(BF))
-        half = 0 if kind == "t" else 1
-        for q in range(4):
-            row_parts[half, pl.ds(q * 32 + (at * 2 + ax) * 8, 8), :] = rows[8 * q:8 * q + 8]
+        place(0 if kind == "t" else 1, at * 2 + ax, merge(blocks))
 
     def row_copy(half, to, slot):
         return pltpu.make_async_remote_copy(
@@ -173,40 +187,57 @@
     def deliver(half):
         send[half] = dot_nn(pack[...], row_parts[half].astype(BF)).astype(BF).reshape(n_xyz, 16, 128)
 
-        @pl.loop(0, n_xyz - 1)
-        def _(k):
-            row_copy(half, peer(k), me).start()
+        for peer in peers:
+            row_copy(half, peer, me).start()
 
         pltpu.make_async_copy(send.at[half, me], recv.at[half, me], own_sem.at[half]).start()
 
     def collect(half):
         pltpu.make_async_copy(send.at[half, me], recv.at[half, me], own_sem.at[half]).wait()
 
-        @pl.loop(0, n_xyz - 1)
-        def _(k):
-            to = peer(k)
-            row_copy(half, to, to).wait()
+        for peer in peers:
+            row_copy(half, peer, peer).wait()
 
         placed = dot_nn(unpack[...], recv[half].reshape(512, 128))
         for q in range(4):
-            out_ref[:, half * 512 + q * 128:half * 512 + (q + 1) * 128] = placed[q * 64:(q + 1) * 64]
+            out_ref[:, half * 512 + q * 128:half * 512 + (q + 1) * 128] = placed[q * 64:(q + 1) * 64].astype(BF)
 
     nulls_copy.wait()
-    for key in groups:
+    link_copies["s", 1, 1].wait()
+    conjugate_through()
+    pl.semaphore_wait(barrier, n_xyz + 1)
+    halo = {}
+    for name, src, dst, to in (
+        ("w", through.at[0], through.at[1], {"xyz": up}),
+        ("s", nulls_hbm.at[pl.ds(0, 2), 0], sh, {"xyz": down}),
+        ("t0", nulls_hbm.at[0, pl.ds(0, 2)], th.at[pl.ds(0, 2)], {"ta": ta_down}),
+        ("t1", nulls_hbm.at[0, pl.ds(2, 2)], th.at[pl.ds(2, 2)], {"ta": ta_down}),
+        ("r", back.at[0], back.at[1], {"xyz": down}),
+    ):
+        i = len(halo)
+        halo[name] = pltpu.make_async_remote_copy(
+            src, dst, halo_send.at[i], halo_recv.at[i], device_id=to, device_id_type=MESH)
+    for name in ("w", "s", "t0", "t1"):
+        halo[name].start()
+
+    for key in groups[1:]:
         link_copies[key].wait()
     group("t", 0, 0)
     group("t", 0, 1)
     group("s", 0, 0)
     group("s", 1, 0)
-    halo["t", 0].wait()
+    halo["w"].wait()
+    back[0] = merge([blocks_through(aw) for aw in range(8)]).astype(BF)
+    halo["r"].start()
+    halo["t0"].wait()
     group("t", 1, 0)
-    halo["t", 1].wait()
+    halo["t1"].wait()
     group("t", 1, 1)
     deliver(0)
-    halo["s", 0].wait()
+    halo["s"].wait()
     group("s", 0, 1)
-    halo["s", 1].wait()
-    group("s", 1, 1)
+    halo["r"].wait()
+    place(1, 3, back[1].astype(F32))
     deliver(1)
     collect(0)
     collect(1)
@@ -215,7 +246,7 @@
 def on_device(nulls, time_links, space_links, owner_lists):
     result = pl.pallas_call(
         kernel,
-        out_shape=jax.ShapeDtypeStruct((64, 1024), F32),
+        out_shape=jax.ShapeDtypeStruct((64, 1024), BF),
         in_specs=[pl.BlockSpec(memory_space=pl.ANY)] * 3 + [pl.BlockSpec(memory_space=pltpu.VMEM)],
         out_specs=pl.BlockSpec(memory_space=pltpu.VMEM),
         scratch_shapes=[
@@ -223,9 +254,11 @@
             pltpu.VMEM((2, 4, 32, 64, 128), BF),
             pltpu.VMEM((4, 2, 32, 64, 128), BF),
             pltpu.VMEM((4, 32, 16, 128), BF),
-            pltpu.VMEM((4, 32, 16, 128), BF),
+            pltpu.VMEM((2, 32, 16, 128), BF),
             pltpu.VMEM((8, 8, 16, 1024), BF),
             pltpu.VMEM((2, 128, 128), F32),
+            pltpu.VMEM((2, 2, 32, 16, 128), BF),
+            pltpu.VMEM((2, 32, 128), BF),
             pltpu.VMEM((32, 256), BF),
             pltpu.VMEM((512, 128), BF),
             pltpu.VMEM((256, 512), BF),
@@ -233,15 +266,15 @@
             pltpu.VMEM((2, 32, 16, 128), BF),
             pltpu.SemaphoreType.DMA,
             pltpu.SemaphoreType.DMA((8,)),
-            pltpu.SemaphoreType.DMA((4,)),
-            pltpu.SemaphoreType.DMA((4,)),
+            pltpu.SemaphoreType.DMA((5,)),
+            pltpu.SemaphoreType.DMA((5,)),
             pltpu.SemaphoreType.DMA((2, 32)),
             pltpu.SemaphoreType.DMA((2, 32)),
             pltpu.SemaphoreType.DMA((2,)),
         ],
         compiler_params=pltpu.CompilerParams(collective_id=0, has_side_effects=True),
     )(nulls, time_links, space_links, owner_lists)
-    return result[None]
+    return result.astype(F32)[None]
 
 
 def solution(mesh):

time: 37.2 us -> 34 us (0.914)
  Pallas kernels: 35.4 us -> 32.3 us
  local copies, waits for them, and re-layouts: 1.67 us -> 0 us
  other arithmetic: 0 us -> 1.63 us
    pallas_call x1, Pallas kernels: 35.4 us -> 32.3 us  [on_device(): pl.pallas_call(kernel, out_shape=jax.ShapeDtypeStruct((64, 1024), BF), in...]
    unnamed x1 -> x0, local copies, waits for them, and re-layouts: 1.67 us -> none
    broadcast_in_dim x0 -> x1, other arithmetic: none -> 1.63 us  [on_device(): return result.astype(F32)[None]]
where the time goes in v3:
time: 34 us; the launch traced here: 33.9 us
  Pallas kernels  32.3 us (95%)
  other arithmetic  1.63 us (5%)
    pallas_call x1, Pallas kernels, on_device(): pl.pallas_call(kernel, out_shape=jax.ShapeDtypeStruct((64, 1024), BF), in...  32.3 us
    broadcast_in_dim x1, other arithmetic, on_device(): return result.astype(F32)[None]  1.63 us

profile of v3, /device:TPU:2, one launch (start us, length us, event | category | flops | bytes accessed | tf_op | source)
XLA Modules:
  0.0 33.9 jit_solution(2591949297770769824)
XLA Ops:
  0.0 32.3 %shard_map.46 = bf16[64,1024]{1,0:T(8,128)(2,1)} custom-call(bf16[4,4,32,16,128]{4,3,2,1,0:T(8,128)(2,1)} %nulls_hbm.1, bf16[2,4,32,64,128]{4,3,2,1,0:T(8,128)(2,1)} %tl_hbm.1, bf16[4,2,32,64,128]{4,3,2,1,0:T(8,128)(2,1)} %sl_hbm.1, s32[32,64]{1,0:T(8,128)} %owner_ref.1), custom_call_target="tpu_custom_call" | custom-call | tf_op jit(solution)/shard_map/pallas_call | solution.py:247
  32.3 1.6 %bitcast_convert_fusion = f32[1,64,1024]{2,1,0:T(8,128)} fusion(bf16[64,1024]{1,0:T(8,128)(2,1)} %shard_map.46), kind=kLoop, calls=%fused_computation | loop fusion | flops 65536 | bytes 393216 | tf_op jit(solution)/shard_map/broadcast_in_dim | solution.py:277

commit v4 on v3

--- a/solution.py
+++ b/solution.py
@@ -9,6 +9,7 @@
 
 MESH = pl.DeviceIdType.MESH
 NY, NZ = 4, 8
+ABOVE = 6
 BF, F32, I32 = jnp.bfloat16, jnp.float32, jnp.int32
 
 
@@ -35,7 +36,7 @@
 def kernel(
     nulls_hbm, tl_hbm, sl_hbm, owner_ref, out_ref,
     nulls, tl, sl, th, sh, held, row_parts, through, back, group_rows, pack, unpack, send, recv,
-    nulls_sem, link_sem, halo_send, halo_recv, row_send, row_recv, own_sem,
+    link_sem, halo_send, halo_recv, row_send, row_recv, own_sem, met_sem,
 ):
     ta = lax.axis_index("ta")
     me = lax.axis_index("xyz")
@@ -51,37 +52,42 @@
     pl.semaphore_signal(barrier, inc=1, device_id={"ta": ta_down}, device_id_type=MESH)
     pl.semaphore_signal(barrier, inc=1, device_id={"ta": ta_up}, device_id_type=MESH)
 
-    for peer in peers:
+    column = [rows_y[dy] + my_z for dy in (2, 1, 3)]
+    ring = [rows_y[0] + rows_z[dz] for dz in (4, 3, 5, 2, 6, 1, 7)]
+    for peer in [up, down] + ring + column:
         pl.semaphore_signal(barrier, inc=1, device_id={"xyz": peer}, device_id_type=MESH)
 
-    nulls_copy = pltpu.make_async_copy(nulls_hbm, nulls, nulls_sem)
-    nulls_copy.start()
-    groups = [("s", 1, 1), ("t", 0, 0), ("t", 0, 1), ("s", 0, 0), ("s", 1, 0), ("t", 1, 0), ("t", 1, 1), ("s", 0, 1)]
-    link_copies = {}
-    for i, (kind, at, ax) in enumerate(groups):
-        if kind == "t":
-            src, dst = tl_hbm.at[at, pl.ds(2 * ax, 2)], tl.at[at, pl.ds(2 * ax, 2)]
-        else:
-            src, dst = sl_hbm.at[pl.ds(2 * at, 2), ax], sl.at[pl.ds(2 * at, 2), ax]
-        link_copies[kind, at, ax] = pltpu.make_async_copy(src, dst, link_sem.at[i])
-        link_copies[kind, at, ax].start()
-
-    row, col = iota((32, 256), 0), iota((32, 256), 1)
-    group_rows[...] = one_hot(((row % 8) == (col // 32)) & ((row // 8) == ((col // 8) % 4)))
-    lists = owner_ref[...]
-    wide = jnp.broadcast_to(lists[:, None, :], (32, 16, 64)).reshape(512, 64)
-    base = me * 32
-    first = jnp.sum(jnp.where((wide >= 0) & (wide < base), 1, 0), axis=1, keepdims=True)
-    r512 = iota((512, 1), 0)
-    agg = jnp.sum(jnp.where(iota((512, 64), 1) == first + r512 % 4, wide, 0), axis=1, keepdims=True) - base
-    target = jnp.where((agg >= 0) & (agg < 32), ((r512 // 4) % 4) * 32 + agg, -1)
-    pack[...] = one_hot(iota((512, 128), 1) == target)
-    mine = jnp.broadcast_to(owner_ref[pl.ds(me, 1), :], (256, 64))
-    r256 = iota((256, 1), 0)
-    slot = r256 % 64
-    listed = jnp.sum(jnp.where(iota((256, 64), 1) == slot, mine, 0), axis=1, keepdims=True)
-    place = jnp.where(listed >= 0, (listed // 32) * 16 + (r256 // 64) * 4 + slot % 4, -1)
-    unpack[...] = one_hot(iota((256, 512), 1) == place)
+    def greet():
+        for peer in column:
+            pl.semaphore_signal(met_sem, inc=1, device_id={"xyz": peer}, device_id_type=MESH)
+
+    copies = []
+
+    def fetch(src, dst):
+        copies.append(pltpu.make_async_copy(src, dst, link_sem.at[len(copies)]))
+        copies[-1].start()
+
+    cut = 4 * ABOVE
+    fetch(nulls_hbm.at[pl.ds(2, 2), 3], nulls.at[pl.ds(2, 2), 3])
+    fetch(sl_hbm.at[pl.ds(2, 2), 1, pl.ds(0, cut)], sl.at[pl.ds(2, 2), 1, pl.ds(0, cut)])
+
+    def tables():
+        row, col = iota((32, 256), 0), iota((32, 256), 1)
+        group_rows[...] = one_hot(((row % 8) == (col // 32)) & ((row // 8) == ((col // 8) % 4)))
+        lists = owner_ref[...]
+        wide = jnp.broadcast_to(lists[:, None, :], (32, 16, 64)).reshape(512, 64)
+        base = me * 32
+        first = jnp.sum(jnp.where((wide >= 0) & (wide < base), 1, 0), axis=1, keepdims=True)
+        r512 = iota((512, 1), 0)
+        agg = jnp.sum(jnp.where(iota((512, 64), 1) == first + r512 % 4, wide, 0), axis=1, keepdims=True) - base
+        target = jnp.where((agg >= 0) & (agg < 32), ((r512 // 4) % 4) * 32 + agg, -1)
+        pack[...] = one_hot(iota((512, 128), 1) == target)
+        mine = jnp.broadcast_to(owner_ref[pl.ds(me, 1), :], (256, 64))
+        r256 = iota((256, 1), 0)
+        slot = r256 % 64
+        listed = jnp.sum(jnp.where(iota((256, 64), 1) == slot, mine, 0), axis=1, keepdims=True)
+        place = jnp.where(listed >= 0, (listed // 32) * 16 + (r256 // 64) * 4 + slot % 4, -1)
+        unpack[...] = one_hot(iota((256, 512), 1) == place)
 
     low16 = iota((16, 128), 1) < 64
     low32 = iota((32, 128), 1) < 64
@@ -111,8 +117,8 @@
             yield jnp.concatenate([re, -im], axis=0)
             yield jnp.concatenate([im, re], axis=0)
 
-    def merge(blocks):
-        tiled = dot_nn(jnp.concatenate(blocks, axis=0).astype(BF), spread)
+    def merge(made):
+        tiled = dot_nn(jnp.concatenate(made, axis=0).astype(BF), spread)
         return dot_nn(group_rows[...], jnp.where(keep, tiled, 0.0).astype(BF))
 
     def place(half, part, rows):
@@ -122,7 +128,7 @@
     def conjugate_through():
         zero = jnp.zeros((16, 128), BF)
         for c in range(2):
-            for w in range(0, 32, 4):
+            for w in range(0, cut, 4):
                 rows = []
                 for i in range(4):
                     v = nulls[2 + c, 3, w + i]
@@ -148,6 +154,9 @@
         return dot_nt(jnp.concatenate(left, axis=1), jnp.concatenate(right, axis=1))
 
     def group(kind, at, ax):
+        place(0 if kind == "t" else 1, at * 2 + ax, merge(blocks(kind, at, ax, range(8))))
+
+    def blocks(kind, at, ax, which):
         if kind == "t":
             def links(c, w):
                 return [tl[at, 2 * ax + c, w + i] for i in range(4)]
@@ -167,17 +176,17 @@
             def lowers(c, w):
                 return nulls[2 * at + c, 2 * ax + 1, w]
         slot = (at * 2 + ax) + (0 if kind == "t" else 4)
-        for aw in range(8):
+        for aw in which:
             for c in range(2):
                 for i, image in enumerate(images(c, 4 * aw, links, uppers)):
                     k = (c * 2 + i) * 256
                     held[slot, aw, :, k:k + 128] = image[:16]
                     held[slot, aw, :, k + 128:k + 256] = image[16:]
-        blocks = []
-        for aw in range(8):
+        made = []
+        for aw in which:
             left = jnp.concatenate([x for c in range(2) for x in conjugates(c, 4 * aw, lowers)], axis=1)
-            blocks.append(dot_nt(left, held[slot, aw]))
-        place(0 if kind == "t" else 1, at * 2 + ax, merge(blocks))
+            made.append(dot_nt(left, held[slot, aw]))
+        return made
 
     def row_copy(half, to, slot):
         return pltpu.make_async_remote_copy(
@@ -202,14 +211,12 @@
         for q in range(4):
             out_ref[:, half * 512 + q * 128:half * 512 + (q + 1) * 128] = placed[q * 64:(q + 1) * 64].astype(BF)
 
-    nulls_copy.wait()
-    link_copies["s", 1, 1].wait()
-    conjugate_through()
-    pl.semaphore_wait(barrier, n_xyz + 1)
+    pl.semaphore_wait(barrier, 14)
     halo = {}
     for name, src, dst, to in (
         ("w", through.at[0], through.at[1], {"xyz": up}),
-        ("s", nulls_hbm.at[pl.ds(0, 2), 0], sh, {"xyz": down}),
+        ("s1", nulls_hbm.at[pl.ds(2, 2), 0, pl.ds(cut, 32 - cut)], sh.at[pl.ds(2, 2), pl.ds(cut, 32 - cut)], {"xyz": down}),
+        ("s0", nulls_hbm.at[pl.ds(0, 2), 0], sh.at[pl.ds(0, 2)], {"xyz": down}),
         ("t0", nulls_hbm.at[0, pl.ds(0, 2)], th.at[pl.ds(0, 2)], {"ta": ta_down}),
         ("t1", nulls_hbm.at[0, pl.ds(2, 2)], th.at[pl.ds(2, 2)], {"ta": ta_down}),
         ("r", back.at[0], back.at[1], {"xyz": down}),
@@ -217,27 +224,43 @@
         i = len(halo)
         halo[name] = pltpu.make_async_remote_copy(
             src, dst, halo_send.at[i], halo_recv.at[i], device_id=to, device_id_type=MESH)
-    for name in ("w", "s", "t0", "t1"):
+    for name in ("s1", "s0", "t0", "t1"):
         halo[name].start()
-
-    for key in groups[1:]:
-        link_copies[key].wait()
+    greet()
+    copies[0].wait()
+    copies[1].wait()
+    conjugate_through()
+    halo["w"].start()
+    fetch(nulls_hbm.at[pl.ds(2, 2), pl.ds(0, 3)], nulls.at[pl.ds(2, 2), pl.ds(0, 3)])
+    fetch(nulls_hbm.at[pl.ds(0, 2)], nulls.at[pl.ds(0, 2)])
+    for at in range(2):
+        fetch(tl_hbm.at[at], tl.at[at])
+    fetch(sl_hbm.at[pl.ds(0, 2)], sl.at[pl.ds(0, 2)])
+    fetch(sl_hbm.at[pl.ds(2, 2), 0], sl.at[pl.ds(2, 2), 0])
+    fetch(sl_hbm.at[pl.ds(2, 2), 1, pl.ds(cut, 32 - cut)], sl.at[pl.ds(2, 2), 1, pl.ds(cut, 32 - cut)])
+    tables()
+    for copy in copies[2:]:
+        copy.wait()
     group("t", 0, 0)
     group("t", 0, 1)
     group("s", 0, 0)
     group("s", 1, 0)
+    nil = [jnp.zeros((32, 16), F32)]
     halo["w"].wait()
-    back[0] = merge([blocks_through(aw) for aw in range(8)]).astype(BF)
+    back[0] = merge([blocks_through(aw) for aw in range(ABOVE)] + nil * (8 - ABOVE)).astype(BF)
     halo["r"].start()
     halo["t0"].wait()
     group("t", 1, 0)
     halo["t1"].wait()
     group("t", 1, 1)
+    pl.semaphore_wait(met_sem, 3)
     deliver(0)
-    halo["s"].wait()
+    halo["s1"].wait()
+    own = merge(nil * ABOVE + blocks("s", 1, 1, range(ABOVE, 8)))
+    halo["s0"].wait()
     group("s", 0, 1)
     halo["r"].wait()
-    place(1, 3, back[1].astype(F32))
+    place(1, 3, own + back[1].astype(F32))
     deliver(1)
     collect(0)
     collect(1)
@@ -246,7 +269,7 @@
 def on_device(nulls, time_links, space_links, owner_lists):
     result = pl.pallas_call(
         kernel,
-        out_shape=jax.ShapeDtypeStruct((64, 1024), BF),
+        out_shape=pltpu.VMEM((64, 1024), BF),
         in_specs=[pl.BlockSpec(memory_space=pl.ANY)] * 3 + [pl.BlockSpec(memory_space=pltpu.VMEM)],
         out_specs=pl.BlockSpec(memory_space=pltpu.VMEM),
         scratch_shapes=[
@@ -254,23 +277,23 @@
             pltpu.VMEM((2, 4, 32, 64, 128), BF),
             pltpu.VMEM((4, 2, 32, 64, 128), BF),
             pltpu.VMEM((4, 32, 16, 128), BF),
-            pltpu.VMEM((2, 32, 16, 128), BF),
+            pltpu.VMEM((4, 32, 16, 128), BF),
             pltpu.VMEM((8, 8, 16, 1024), BF),
             pltpu.VMEM((2, 128, 128), F32),
-            pltpu.VMEM((2, 2, 32, 16, 128), BF),
+            pltpu.VMEM((2, 2, 4 * ABOVE, 16, 128), BF),
             pltpu.VMEM((2, 32, 128), BF),
             pltpu.VMEM((32, 256), BF),
             pltpu.VMEM((512, 128), BF),
             pltpu.VMEM((256, 512), BF),
             pltpu.VMEM((2, 32, 16, 128), BF),
             pltpu.VMEM((2, 32, 16, 128), BF),
-            pltpu.SemaphoreType.DMA,
-            pltpu.SemaphoreType.DMA((8,)),
-            pltpu.SemaphoreType.DMA((5,)),
-            pltpu.SemaphoreType.DMA((5,)),
+            pltpu.SemaphoreType.DMA((9,)),
+            pltpu.SemaphoreType.DMA((6,)),
+            pltpu.SemaphoreType.DMA((6,)),
             pltpu.SemaphoreType.DMA((2, 32)),
             pltpu.SemaphoreType.DMA((2, 32)),
             pltpu.SemaphoreType.DMA((2,)),
+            pltpu.SemaphoreType.REGULAR,
         ],
         compiler_params=pltpu.CompilerParams(collective_id=0, has_side_effects=True),
     )(nulls, time_links, space_links, owner_lists)

time: 34 us -> 30.5 us (0.90)
  Pallas kernels: 32.3 us -> 29.4 us
  other arithmetic: 1.63 us -> 0.72 us
    pallas_call x1, Pallas kernels: 32.3 us -> 29.4 us  [on_device(): pl.pallas_call(kernel, out_shape=pltpu.VMEM((64, 1024), BF), in_specs=[pl...]
    broadcast_in_dim x1, other arithmetic: 1.63 us -> 0.72 us  [on_device(): return result.astype(F32)[None]]
where the time goes in v4:
time: 30.5 us; the launch traced here: 30.1 us
  Pallas kernels  29.4 us (96%)
  other arithmetic  0.72 us (2%)
    pallas_call x1, Pallas kernels, on_device(): pl.pallas_call(kernel, out_shape=pltpu.VMEM((64, 1024), BF), in_specs=[pl...  29.4 us
    broadcast_in_dim x1, other arithmetic, on_device(): return result.astype(F32)[None]  0.72 us

profile of v4, /device:TPU:2, one launch (start us, length us, event | category | flops | bytes accessed | tf_op | source)
XLA Modules:
  0.0 30.1 jit_solution(14091495035717930628)
XLA Ops:
  0.0 29.4 %shard_map.46 = bf16[64,1024]{1,0:T(8,128)(2,1)S(1)} custom-call(bf16[4,4,32,16,128]{4,3,2,1,0:T(8,128)(2,1)} %nulls_hbm.1, bf16[2,4,32,64,128]{4,3,2,1,0:T(8,128)(2,1)} %tl_hbm.1, bf16[4,2,32,64,128]{4,3,2,1,0:T(8,128)(2,1)} %sl_hbm.1, s32[32,64]{1,0:T(8,128)} %owner_ref.1), custom_call_target="tpu_custom_call" | custom-call | tf_op jit(solution)/shard_map/pallas_call | solution.py:270
  29.4 0.7 %bitcast_convert_fusion = f32[1,64,1024]{2,1,0:T(8,128)} fusion(bf16[64,1024]{1,0:T(8,128)(2,1)S(1)} %shard_map.46), kind=kLoop, calls=%fused_computation | loop fusion | flops 65536 | bytes 393216 | tf_op jit(solution)/shard_map/broadcast_in_dim | solution.py:300

commit v5 on v4

--- a/solution.py
+++ b/solution.py
@@ -36,7 +36,7 @@
 def kernel(
     nulls_hbm, tl_hbm, sl_hbm, owner_ref, out_ref,
     nulls, tl, sl, th, sh, held, row_parts, through, back, group_rows, pack, unpack, send, recv,
-    link_sem, halo_send, halo_recv, row_send, row_recv, own_sem, met_sem,
+    link_sem, halo_send, halo_recv, row_send, row_recv, met_sem,
 ):
     ta = lax.axis_index("ta")
     me = lax.axis_index("xyz")
@@ -71,23 +71,31 @@
     fetch(nulls_hbm.at[pl.ds(2, 2), 3], nulls.at[pl.ds(2, 2), 3])
     fetch(sl_hbm.at[pl.ds(2, 2), 1, pl.ds(0, cut)], sl.at[pl.ds(2, 2), 1, pl.ds(0, cut)])
 
-    def tables():
+    def packing():
         row, col = iota((32, 256), 0), iota((32, 256), 1)
         group_rows[...] = one_hot(((row % 8) == (col // 32)) & ((row // 8) == ((col // 8) % 4)))
         lists = owner_ref[...]
-        wide = jnp.broadcast_to(lists[:, None, :], (32, 16, 64)).reshape(512, 64)
         base = me * 32
-        first = jnp.sum(jnp.where((wide >= 0) & (wide < base), 1, 0), axis=1, keepdims=True)
-        r512 = iota((512, 1), 0)
-        agg = jnp.sum(jnp.where(iota((512, 64), 1) == first + r512 % 4, wide, 0), axis=1, keepdims=True) - base
-        target = jnp.where((agg >= 0) & (agg < 32), ((r512 // 4) % 4) * 32 + agg, -1)
-        pack[...] = one_hot(iota((512, 128), 1) == target)
-        mine = jnp.broadcast_to(owner_ref[pl.ds(me, 1), :], (256, 64))
-        r256 = iota((256, 1), 0)
-        slot = r256 % 64
-        listed = jnp.sum(jnp.where(iota((256, 64), 1) == slot, mine, 0), axis=1, keepdims=True)
-        place = jnp.where(listed >= 0, (listed // 32) * 16 + (r256 // 64) * 4 + slot % 4, -1)
-        unpack[...] = one_hot(iota((256, 512), 1) == place)
+        place = iota((32, 64), 1)
+        first = jnp.sum(jnp.where((lists >= 0) & (lists < base), 1, 0), axis=1, keepdims=True)
+        lane = iota((32, 128), 1)
+        picks = []
+        for r in range(4):
+            agg = jnp.sum(jnp.where(place == first + r, lists, 0), axis=1, keepdims=True) - base
+            picks.append(one_hot((lane % 32 == agg) & (agg >= 0) & (agg < 32)))
+        row, col = iota((512, 128), 0), iota((512, 128), 1)
+        spreader = one_hot((row // 16 == col % 32) & (row % 4 == col // 32))
+        wide = dot_nn(spreader, jnp.concatenate(picks, axis=0))
+        pack[...] = jnp.where((row // 4) % 4 == col // 32, wide, 0.0).astype(BF)
+
+    def unpacking():
+        mine = jnp.broadcast_to(owner_ref[pl.ds(me, 1), :], (64, 64))
+        r64 = iota((64, 1), 0)
+        listed = jnp.sum(jnp.where(iota((64, 64), 1) == r64, mine, 0), axis=1, keepdims=True)
+        place = jnp.where(listed >= 0, (listed // 32) * 16 + r64 % 4, -4 * 16)
+        col = iota((64, 512), 1)
+        for q in range(4):
+            unpack[pl.ds(64 * q, 64), :] = one_hot(col == place + 4 * q)
 
     low16 = iota((16, 128), 1) < 64
     low32 = iota((32, 128), 1) < 64
@@ -188,29 +196,28 @@
             made.append(dot_nt(left, held[slot, aw]))
         return made
 
-    def row_copy(half, to, slot):
-        return pltpu.make_async_remote_copy(
-            send.at[half, to], recv.at[half, me], row_send.at[half, to], row_recv.at[half, slot],
-            device_id={"xyz": to}, device_id_type=MESH)
-
     def deliver(half):
         send[half] = dot_nn(pack[...], row_parts[half].astype(BF)).astype(BF).reshape(n_xyz, 16, 128)
-
         for peer in peers:
-            row_copy(half, peer, me).start()
-
-        pltpu.make_async_copy(send.at[half, me], recv.at[half, me], own_sem.at[half]).start()
+            pltpu.make_async_remote_copy(
+                send.at[half, peer], recv.at[half, me], row_send.at[half], row_recv.at[half],
+                device_id={"xyz": peer}, device_id_type=MESH).start()
+        pltpu.make_async_copy(send.at[half, me], recv.at[half, me], row_recv.at[half]).start()
 
     def collect(half):
-        pltpu.make_async_copy(send.at[half, me], recv.at[half, me], own_sem.at[half]).wait()
-
-        for peer in peers:
-            row_copy(half, peer, peer).wait()
-
+        pltpu.make_async_copy(recv.at[half], recv.at[half], row_recv.at[half]).wait()
         placed = dot_nn(unpack[...], recv[half].reshape(512, 128))
         for q in range(4):
             out_ref[:, half * 512 + q * 128:half * 512 + (q + 1) * 128] = placed[q * 64:(q + 1) * 64].astype(BF)
 
+    fetch(nulls_hbm.at[pl.ds(0, 2)], nulls.at[pl.ds(0, 2)])
+    fetch(nulls_hbm.at[pl.ds(2, 2), pl.ds(0, 3)], nulls.at[pl.ds(2, 2), pl.ds(0, 3)])
+    fetch(tl_hbm.at[0], tl.at[0])
+    fetch(sl_hbm.at[pl.ds(0, 2), 0], sl.at[pl.ds(0, 2), 0])
+    fetch(sl_hbm.at[pl.ds(2, 2), 0], sl.at[pl.ds(2, 2), 0])
+    fetch(tl_hbm.at[1], tl.at[1])
+    fetch(sl_hbm.at[pl.ds(0, 2), 1], sl.at[pl.ds(0, 2), 1])
+    fetch(sl_hbm.at[pl.ds(2, 2), 1, pl.ds(cut, 32 - cut)], sl.at[pl.ds(2, 2), 1, pl.ds(cut, 32 - cut)])
     pl.semaphore_wait(barrier, 14)
     halo = {}
     for name, src, dst, to in (
@@ -231,30 +238,28 @@
     copies[1].wait()
     conjugate_through()
     halo["w"].start()
-    fetch(nulls_hbm.at[pl.ds(2, 2), pl.ds(0, 3)], nulls.at[pl.ds(2, 2), pl.ds(0, 3)])
-    fetch(nulls_hbm.at[pl.ds(0, 2)], nulls.at[pl.ds(0, 2)])
-    for at in range(2):
-        fetch(tl_hbm.at[at], tl.at[at])
-    fetch(sl_hbm.at[pl.ds(0, 2)], sl.at[pl.ds(0, 2)])
-    fetch(sl_hbm.at[pl.ds(2, 2), 0], sl.at[pl.ds(2, 2), 0])
-    fetch(sl_hbm.at[pl.ds(2, 2), 1, pl.ds(cut, 32 - cut)], sl.at[pl.ds(2, 2), 1, pl.ds(cut, 32 - cut)])
-    tables()
-    for copy in copies[2:]:
+    packing()
+    for copy in copies[2:5]:
         copy.wait()
     group("t", 0, 0)
     group("t", 0, 1)
+    copies[5].wait()
+    copies[6].wait()
     group("s", 0, 0)
     group("s", 1, 0)
     nil = [jnp.zeros((32, 16), F32)]
     halo["w"].wait()
     back[0] = merge([blocks_through(aw) for aw in range(ABOVE)] + nil * (8 - ABOVE)).astype(BF)
     halo["r"].start()
+    copies[7].wait()
     halo["t0"].wait()
+    halo["t1"].wait()
     group("t", 1, 0)
-    halo["t1"].wait()
     group("t", 1, 1)
     pl.semaphore_wait(met_sem, 3)
     deliver(0)
+    copies[8].wait()
+    copies[9].wait()
     halo["s1"].wait()
     own = merge(nil * ABOVE + blocks("s", 1, 1, range(ABOVE, 8)))
     halo["s0"].wait()
@@ -262,8 +267,12 @@
     halo["r"].wait()
     place(1, 3, own + back[1].astype(F32))
     deliver(1)
+    unpacking()
     collect(0)
     collect(1)
+    for half in range(2):
+        most = send.at[half, pl.ds(0, n_xyz - 1)]
+        pltpu.make_async_copy(most, most, row_send.at[half]).wait()
 
 
 def on_device(nulls, time_links, space_links, owner_lists):
@@ -287,11 +296,10 @@
             pltpu.VMEM((256, 512), BF),
             pltpu.VMEM((2, 32, 16, 128), BF),
             pltpu.VMEM((2, 32, 16, 128), BF),
-            pltpu.SemaphoreType.DMA((9,)),
+            pltpu.SemaphoreType.DMA((10,)),
             pltpu.SemaphoreType.DMA((6,)),
             pltpu.SemaphoreType.DMA((6,)),
-            pltpu.SemaphoreType.DMA((2, 32)),
-            pltpu.SemaphoreType.DMA((2, 32)),
+            pltpu.SemaphoreType.DMA((2,)),
             pltpu.SemaphoreType.DMA((2,)),
             pltpu.SemaphoreType.REGULAR,
         ],

time: 30.5 us -> 29.8 us (0.977)
  the two profiles are of different devices: /device:TPU:2 before, /device:TPU:1 now
where the time goes in v5:
time: 29.8 us; the launch traced here: 29.6 us
  Pallas kernels  28.9 us (97%)
  other arithmetic  0.72 us (2%)
    pallas_call x1, Pallas kernels, on_device(): pl.pallas_call(kernel, out_shape=pltpu.VMEM((64, 1024), BF), in_specs=[pl...  28.9 us
    broadcast_in_dim x1, other arithmetic, on_device(): return result.astype(F32)[None]  0.72 us

profile of v5, /device:TPU:1, one launch (start us, length us, event | category | flops | bytes accessed | tf_op | source)
XLA Modules:
  0.0 29.6 jit_solution(11291833271247594797)
XLA Ops:
  0.0 28.9 %shard_map.46 = bf16[64,1024]{1,0:T(8,128)(2,1)S(1)} custom-call(bf16[4,4,32,16,128]{4,3,2,1,0:T(8,128)(2,1)} %nulls_hbm.1, bf16[2,4,32,64,128]{4,3,2,1,0:T(8,128)(2,1)} %tl_hbm.1, bf16[4,2,32,64,128]{4,3,2,1,0:T(8,128)(2,1)} %sl_hbm.1, s32[32,64]{1,0:T(8,128)} %owner_ref.1), custom_call_target="tpu_custom_call" | custom-call | tf_op jit(solution)/shard_map/pallas_call | solution.py:279
  28.9 0.7 %bitcast_convert_fusion = f32[1,64,1024]{2,1,0:T(8,128)} fusion(bf16[64,1024]{1,0:T(8,128)(2,1)S(1)} %shard_map.46), kind=kLoop, calls=%fused_computation | loop fusion | flops 65536 | bytes 393216 | tf_op jit(solution)/shard_map/broadcast_in_dim | solution.py:308

commit v6 on v5

--- a/solution.py
+++ b/solution.py
@@ -53,23 +53,37 @@
     pl.semaphore_signal(barrier, inc=1, device_id={"ta": ta_up}, device_id_type=MESH)
 
     column = [rows_y[dy] + my_z for dy in (2, 1, 3)]
-    ring = [rows_y[0] + rows_z[dz] for dz in (4, 3, 5, 2, 6, 1, 7)]
+    ring = [rows_y[0] + rows_z[dz] for dz in (2, 6, 1, 7)]
     for peer in [up, down] + ring + column:
         pl.semaphore_signal(barrier, inc=1, device_id={"xyz": peer}, device_id_type=MESH)
 
-    def greet():
-        for peer in column:
-            pl.semaphore_signal(met_sem, inc=1, device_id={"xyz": peer}, device_id_type=MESH)
-
-    copies = []
-
-    def fetch(src, dst):
-        copies.append(pltpu.make_async_copy(src, dst, link_sem.at[len(copies)]))
-        copies[-1].start()
+    def greet(level):
+        for peer in column + (ring[:2] if level == 0 else []):
+            pl.semaphore_signal(met_sem.at[level], inc=1, device_id={"xyz": peer}, device_id_type=MESH)
+
+    loads = {}
+
+    def fetch(name, src, dst):
+        loads[name] = pltpu.make_async_copy(src, dst, link_sem.at[len(loads)])
+        loads[name].start()
 
     cut = 4 * ABOVE
-    fetch(nulls_hbm.at[pl.ds(2, 2), 3], nulls.at[pl.ds(2, 2), 3])
-    fetch(sl_hbm.at[pl.ds(2, 2), 1, pl.ds(0, cut)], sl.at[pl.ds(2, 2), 1, pl.ds(0, cut)])
+    early, late = pl.ds(0, cut), pl.ds(cut, 32 - cut)
+    low, high = pl.ds(0, 2), pl.ds(2, 2)
+    fetch("n0", nulls_hbm.at[high, 3], nulls.at[high, 3])
+    fetch("s11", sl_hbm.at[high, 1, early], sl.at[high, 1, early])
+    fetch("n1", nulls_hbm.at[3, 2], nulls.at[3, 2])
+    fetch("t11", tl_hbm.at[1, high, early], tl.at[1, high, early])
+    fetch("n2", nulls_hbm.at[low], nulls.at[low])
+    fetch("n3", nulls_hbm.at[high, low], nulls.at[high, low])
+    fetch("n4", nulls_hbm.at[2, 2], nulls.at[2, 2])
+    fetch("t0", tl_hbm.at[0], tl.at[0])
+    fetch("s00", sl_hbm.at[low, 0], sl.at[low, 0])
+    fetch("s10", sl_hbm.at[high, 0], sl.at[high, 0])
+    fetch("t10", tl_hbm.at[1, low], tl.at[1, low])
+    fetch("s01", sl_hbm.at[low, 1], sl.at[low, 1])
+    fetch("t11b", tl_hbm.at[1, high, late], tl.at[1, high, late])
+    fetch("s11b", sl_hbm.at[high, 1, late], sl.at[high, 1, late])
 
     def packing():
         row, col = iota((32, 256), 0), iota((32, 256), 1)
@@ -133,32 +147,33 @@
         for q in range(4):
             row_parts[half, pl.ds(q * 32 + part * 8, 8), :] = rows[8 * q:8 * q + 8]
 
-    def conjugate_through():
+    def conjugate_through(half):
         zero = jnp.zeros((16, 128), BF)
         for c in range(2):
             for w in range(0, cut, 4):
                 rows = []
                 for i in range(4):
-                    v = nulls[2 + c, 3, w + i]
+                    v = nulls[2 + c, 3, w + i] if half else nulls[3, 2 + c, w + i]
                     t = swap_halves(v)
                     if i % 2 == 0:
                         part = jnp.concatenate([jnp.where(low16, v, zero), jnp.where(low16, t, zero)], axis=0)
                     else:
                         part = jnp.concatenate([jnp.where(low16, zero, t), jnp.where(low16, zero, v)], axis=0)
                     rows.append(jnp.concatenate([part, none] if i < 2 else [none, part], axis=1))
-                weights = jnp.concatenate([sl[2 + c, 1, w + i] for i in range(4)], axis=0)
+                mats = [sl[2 + c, 1, w + i] if half else tl[1, 2 + c, w + i] for i in range(4)]
+                weights = jnp.concatenate(mats, axis=0)
                 product = dot_nn(jnp.concatenate(rows, axis=0), weights)
                 for i in range(4):
                     top, low = product[32 * i:32 * i + 16], product[32 * i + 16:32 * i + 32]
-                    through[0, c, w + i] = (top + jnp.where(low16, swap_halves(low), -swap_halves(low))).astype(BF)
-
-    def blocks_through(aw):
+                    through[half, 0, c, w + i] = (top + jnp.where(low16, swap_halves(low), -swap_halves(low))).astype(BF)
+
+    def blocks_through(half, aw):
         left, right = [], []
         for c in range(2):
             for w in range(4 * aw, 4 * aw + 4):
-                v = through[1, c, w]
+                v = through[half, 1, c, w]
                 left.append(jnp.concatenate([v * turn, swap_halves(v)], axis=0))
-                right.append(nulls[2 + c, 0, w])
+                right.append(nulls[2 + c, 0, w] if half else nulls[0, 2 + c, w])
         return dot_nt(jnp.concatenate(left, axis=1), jnp.concatenate(right, axis=1))
 
     def group(kind, at, ax):
@@ -210,62 +225,69 @@
         for q in range(4):
             out_ref[:, half * 512 + q * 128:half * 512 + (q + 1) * 128] = placed[q * 64:(q + 1) * 64].astype(BF)
 
-    fetch(nulls_hbm.at[pl.ds(0, 2)], nulls.at[pl.ds(0, 2)])
-    fetch(nulls_hbm.at[pl.ds(2, 2), pl.ds(0, 3)], nulls.at[pl.ds(2, 2), pl.ds(0, 3)])
-    fetch(tl_hbm.at[0], tl.at[0])
-    fetch(sl_hbm.at[pl.ds(0, 2), 0], sl.at[pl.ds(0, 2), 0])
-    fetch(sl_hbm.at[pl.ds(2, 2), 0], sl.at[pl.ds(2, 2), 0])
-    fetch(tl_hbm.at[1], tl.at[1])
-    fetch(sl_hbm.at[pl.ds(0, 2), 1], sl.at[pl.ds(0, 2), 1])
-    fetch(sl_hbm.at[pl.ds(2, 2), 1, pl.ds(cut, 32 - cut)], sl.at[pl.ds(2, 2), 1, pl.ds(cut, 32 - cut)])
-    pl.semaphore_wait(barrier, 14)
+    pl.semaphore_wait(barrier, 11)
     halo = {}
     for name, src, dst, to in (
-        ("w", through.at[0], through.at[1], {"xyz": up}),
-        ("s1", nulls_hbm.at[pl.ds(2, 2), 0, pl.ds(cut, 32 - cut)], sh.at[pl.ds(2, 2), pl.ds(cut, 32 - cut)], {"xyz": down}),
-        ("s0", nulls_hbm.at[pl.ds(0, 2), 0], sh.at[pl.ds(0, 2)], {"xyz": down}),
-        ("t0", nulls_hbm.at[0, pl.ds(0, 2)], th.at[pl.ds(0, 2)], {"ta": ta_down}),
-        ("t1", nulls_hbm.at[0, pl.ds(2, 2)], th.at[pl.ds(2, 2)], {"ta": ta_down}),
-        ("r", back.at[0], back.at[1], {"xyz": down}),
+        ("t0", nulls_hbm.at[0, low], th.at[low], {"ta": ta_down}),
+        ("t1", nulls_hbm.at[0, high, late], th.at[high, late], {"ta": ta_down}),
+        ("s1", nulls_hbm.at[high, 0, late], sh.at[high, late], {"xyz": down}),
+        ("s0", nulls_hbm.at[low, 0], sh.at[low], {"xyz": down}),
+        ("ws", through.at[1, 0], through.at[1, 1], {"xyz": up}),
+        ("wt", through.at[0, 0], through.at[0, 1], {"ta": ta_up}),
+        ("rs", back.at[1, 0], back.at[1, 1], {"xyz": down}),
+        ("rt", back.at[0, 0], back.at[0, 1], {"ta": ta_down}),
     ):
         i = len(halo)
         halo[name] = pltpu.make_async_remote_copy(
             src, dst, halo_send.at[i], halo_recv.at[i], device_id=to, device_id_type=MESH)
-    for name in ("s1", "s0", "t0", "t1"):
+    for name in ("t0", "s1", "t1", "s0"):
         halo[name].start()
-    greet()
-    copies[0].wait()
-    copies[1].wait()
-    conjugate_through()
-    halo["w"].start()
+    greet(0)
+    loads["n0"].wait()
+    loads["s11"].wait()
+    conjugate_through(1)
+    halo["ws"].start()
+    loads["n1"].wait()
+    loads["t11"].wait()
+    conjugate_through(0)
+    halo["wt"].start()
+    pl.semaphore_wait(met_sem.at[0], 5)
+    greet(1)
     packing()
-    for copy in copies[2:5]:
-        copy.wait()
+    for name in ("n2", "n3", "n4", "t0"):
+        loads[name].wait()
     group("t", 0, 0)
     group("t", 0, 1)
-    copies[5].wait()
-    copies[6].wait()
+    loads["s00"].wait()
+    loads["s10"].wait()
     group("s", 0, 0)
     group("s", 1, 0)
     nil = [jnp.zeros((32, 16), F32)]
-    halo["w"].wait()
-    back[0] = merge([blocks_through(aw) for aw in range(ABOVE)] + nil * (8 - ABOVE)).astype(BF)
-    halo["r"].start()
-    copies[7].wait()
+    rest = range(ABOVE, 8)
+    loads["t10"].wait()
+    loads["t11b"].wait()
+    loads["s11b"].wait()
+    loads["s01"].wait()
+    halo["wt"].wait()
+    back[0, 0] = merge([blocks_through(0, aw) for aw in range(ABOVE)] + nil * (8 - ABOVE)).astype(BF)
+    halo["rt"].start()
     halo["t0"].wait()
+    group("t", 1, 0)
+    halo["ws"].wait()
+    back[1, 0] = merge([blocks_through(1, aw) for aw in range(ABOVE)] + nil * (8 - ABOVE)).astype(BF)
+    halo["rs"].start()
     halo["t1"].wait()
-    group("t", 1, 0)
-    group("t", 1, 1)
-    pl.semaphore_wait(met_sem, 3)
+    halo["s1"].wait()
+    own_t = merge(nil * ABOVE + blocks("t", 1, 1, rest))
+    own_s = merge(nil * ABOVE + blocks("s", 1, 1, rest))
+    halo["rt"].wait()
+    place(0, 3, own_t + back[0, 1].astype(F32))
+    pl.semaphore_wait(met_sem.at[1], 3)
     deliver(0)
-    copies[8].wait()
-    copies[9].wait()
-    halo["s1"].wait()
-    own = merge(nil * ABOVE + blocks("s", 1, 1, range(ABOVE, 8)))
     halo["s0"].wait()
     group("s", 0, 1)
-    halo["r"].wait()
-    place(1, 3, own + back[1].astype(F32))
+    halo["rs"].wait()
+    place(1, 3, own_s + back[1, 1].astype(F32))
     deliver(1)
     unpacking()
     collect(0)
@@ -289,19 +311,19 @@
             pltpu.VMEM((4, 32, 16, 128), BF),
             pltpu.VMEM((8, 8, 16, 1024), BF),
             pltpu.VMEM((2, 128, 128), F32),
-            pltpu.VMEM((2, 2, 4 * ABOVE, 16, 128), BF),
-            pltpu.VMEM((2, 32, 128), BF),
+            pltpu.VMEM((2, 2, 2, 4 * ABOVE, 16, 128), BF),
+            pltpu.VMEM((2, 2, 32, 128), BF),
             pltpu.VMEM((32, 256), BF),
             pltpu.VMEM((512, 128), BF),
             pltpu.VMEM((256, 512), BF),
             pltpu.VMEM((2, 32, 16, 128), BF),
             pltpu.VMEM((2, 32, 16, 128), BF),
-            pltpu.SemaphoreType.DMA((10,)),
-            pltpu.SemaphoreType.DMA((6,)),
-            pltpu.SemaphoreType.DMA((6,)),
+            pltpu.SemaphoreType.DMA((14,)),
+            pltpu.SemaphoreType.DMA((8,)),
+            pltpu.SemaphoreType.DMA((8,)),
             pltpu.SemaphoreType.DMA((2,)),
             pltpu.SemaphoreType.DMA((2,)),
-            pltpu.SemaphoreType.REGULAR,
+            pltpu.SemaphoreType.REGULAR((2,)),
         ],
         compiler_params=pltpu.CompilerParams(collective_id=0, has_side_effects=True),
     )(nulls, time_links, space_links, owner_lists)

time: 29.8 us -> 28.6 us (0.960)
  the two profiles are of different devices: /device:TPU:1 before, /device:TPU:2 now
where the time goes in v6:
time: 28.6 us; the launch traced here: 28.3 us
  Pallas kernels  27.6 us (97%)
  other arithmetic  0.72 us (3%)
    pallas_call x1, Pallas kernels, on_device(): pl.pallas_call(kernel, out_shape=pltpu.VMEM((64, 1024), BF), in_specs=[pl...  27.6 us
    broadcast_in_dim x1, other arithmetic, on_device(): return result.astype(F32)[None]  0.72 us

profile of v6, /device:TPU:2, one launch (start us, length us, event | category | flops | bytes accessed | tf_op | source)
XLA Modules:
  0.0 28.3 jit_solution(6422591084168038406)
XLA Ops:
  0.0 27.6 %shard_map.46 = bf16[64,1024]{1,0:T(8,128)(2,1)S(1)} custom-call(bf16[4,4,32,16,128]{4,3,2,1,0:T(8,128)(2,1)} %nulls_hbm.1, bf16[2,4,32,64,128]{4,3,2,1,0:T(8,128)(2,1)} %tl_hbm.1, bf16[4,2,32,64,128]{4,3,2,1,0:T(8,128)(2,1)} %sl_hbm.1, s32[32,64]{1,0:T(8,128)} %owner_ref.1), custom_call_target="tpu_custom_call" | custom-call | tf_op jit(solution)/shard_map/pallas_call | solution.py:301
  27.6 0.7 %bitcast_convert_fusion = f32[1,64,1024]{2,1,0:T(8,128)} fusion(bf16[64,1024]{1,0:T(8,128)(2,1)S(1)} %shard_map.46), kind=kLoop, calls=%fused_computation | loop fusion | flops 65536 | bytes 393216 | tf_op jit(solution)/shard_map/broadcast_in_dim | solution.py:330

commit v7 on v6

--- a/solution.py
+++ b/solution.py
@@ -225,6 +225,7 @@
         for q in range(4):
             out_ref[:, half * 512 + q * 128:half * 512 + (q + 1) * 128] = placed[q * 64:(q + 1) * 64].astype(BF)
 
+    packing()
     pl.semaphore_wait(barrier, 11)
     halo = {}
     for name, src, dst, to in (
@@ -253,7 +254,6 @@
     halo["wt"].start()
     pl.semaphore_wait(met_sem.at[0], 5)
     greet(1)
-    packing()
     for name in ("n2", "n3", "n4", "t0"):
         loads[name].wait()
     group("t", 0, 0)

time: 28.6 us -> 28.3 us (0.990)
  Pallas kernels: 27.6 us -> 27.1 us
    pallas_call x1, Pallas kernels: 27.6 us -> 27.1 us  [on_device(): pl.pallas_call(kernel, out_shape=pltpu.VMEM((64, 1024), BF), in_specs=[pl...]
where the time goes in v7:
time: 28.3 us; the launch traced here: 27.9 us
  Pallas kernels  27.1 us (96%)
  other arithmetic  0.72 us (3%)
    pallas_call x1, Pallas kernels, on_device(): pl.pallas_call(kernel, out_shape=pltpu.VMEM((64, 1024), BF), in_specs=[pl...  27.1 us
    broadcast_in_dim x1, other arithmetic, on_device(): return result.astype(F32)[None]  0.72 us

profile of v7, /device:TPU:2, one launch (start us, length us, event | category | flops | bytes accessed | tf_op | source)
XLA Modules:
  0.0 27.9 jit_solution(14986277496294509204)
XLA Ops:
  0.0 27.1 %shard_map.46 = bf16[64,1024]{1,0:T(8,128)(2,1)S(1)} custom-call(bf16[4,4,32,16,128]{4,3,2,1,0:T(8,128)(2,1)} %nulls_hbm.1, bf16[2,4,32,64,128]{4,3,2,1,0:T(8,128)(2,1)} %tl_hbm.1, bf16[4,2,32,64,128]{4,3,2,1,0:T(8,128)(2,1)} %sl_hbm.1, s32[32,64]{1,0:T(8,128)} %owner_ref.1), custom_call_target="tpu_custom_call" | custom-call | tf_op jit(solution)/shard_map/pallas_call | solution.py:301
  27.1 0.7 %bitcast_convert_fusion = f32[1,64,1024]{2,1,0:T(8,128)} fusion(bf16[64,1024]{1,0:T(8,128)(2,1)S(1)} %shard_map.46), kind=kLoop, calls=%fused_computation | loop fusion | flops 65536 | bytes 393216 | tf_op jit(solution)/shard_map/broadcast_in_dim | solution.py:330
